TPU v7x, 128 devices: a whole 4x4x4 slice. The times are simulated.
128 devices in a mesh: slot: 16 (over y, z), head: 2 (over x_lo), conv: 4 (over x_hi, core).
Axes of the slice: x: 4 (x_hi: 2, x_lo: 2; x = x_hi * 2 + x_lo), y: 4, z: 4, core: 2. Of those that a mesh axis runs over, the one named last changes fastest.
Arguments:
- queries: bfloat16 [1024, 64, 128], P(('conv', 'slot'), 'head'), may hold values from -96 to 96
- out_grad: bfloat16 [1024, 64, 128], P(('conv', 'slot'), 'head'), may hold values from -768 to 768
- row_positions: int32 [1024], P('conv'), may hold values from 0 to 8191
- slot_offsets: int32 [16384], P('slot'), may hold values from 0 to 16382, as said below
- cache: float32 [2, 16384, 4, 128], P(None, 'slot', 'head'), may hold values from -12 to 12
- first_moment: float32 [2, 16384, 4, 128], P(None, 'slot', 'head'), may hold values from -6 to 6
- second_moment: float32 [2, 16384, 4, 128], P(None, 'slot', 'head'), may hold values from 0.01 to 1000
Outputs:
- new_cache: float32 [2, 16384, 4, 128], P(None, 'slot', 'head')
- new_first_moment: float32 [2, 16384, 4, 128], P(None, 'slot', 'head')
- new_second_moment: float32 [2, 16384, 4, 128], P(None, 'slot', 'head')
- query_grad: float32 [1024, 64, 128], P(('conv', 'slot'), 'head')
Inputs may be any that keep to these rules, and one draw needn't show every extreme that they name: `slot_offsets`: never falls from one slot to the next; its first two entries are 0.
All inputs are finite; a program needn't handle non-finite values.
Results may differ from a plain program's by a relative error of at most 0.012.
The roundings to bfloat16 on the way count: a program that leaves them out, or rounds other values in their place, can miss the bound.
Values may be sent and summed in bfloat16 or wider, within the bound.
A program may use at most 128 MiB of HBM per device.

v0:
```python
import math
import jax
import jax.numpy as jnp
from jax import lax
from jax.sharding import PartitionSpec as P

STEP = 20
learn_rate = 0.01
beta_one = 0.9
beta_two = 0.95
adam_eps = 1e-08
masked_score = -1e30


def merged(x, axis, combine):
    everything = jax.tree.map(lambda part: lax.all_gather(part, axis), x)
    leading = jax.tree.map(lambda part: part[0], everything)

    def lap(k, so_far):
        return combine(so_far, jax.tree.map(lambda part: part[k], everything))

    return lax.fori_loop(1, lax.axis_size(axis), lap, leading)


def merge_pairs(earlier, later):
    largest = jnp.maximum(earlier[0], later[0])
    return (
        largest,
        earlier[1] * jnp.exp(earlier[0] - largest) + later[1] * jnp.exp(later[0] - largest),
    )


def local(queries, out_grad, row_positions, slot_offsets, cache, first_moment, second_moment):
    query_all, grad_all = (
        lax.all_gather(queries, "slot", axis=0, tiled=True),
        lax.all_gather(out_grad, "slot", axis=0, tiled=True),
    )
    total_rows, head_count, head_width = query_all.shape
    kv_count = cache.shape[2]
    group_heads = head_count // kv_count
    score_scale = 1.0 / math.sqrt(head_width)
    block_rows = min(64, total_rows)
    block_count = total_rows // block_rows
    key_half = cache[0].astype(jnp.bfloat16)
    value_half = cache[1].astype(jnp.bfloat16)
    query_blocks = query_all.reshape(block_count, block_rows, kv_count, group_heads, head_width)
    grad_blocks = grad_all.reshape(block_count, block_rows, kv_count, group_heads, head_width)
    visible_all = (slot_offsets[None, :] <= row_positions[:, None]).reshape(
        block_count, block_rows, -1
    )

    def masked_scores(query_block, visible):
        raw_score = (
            jnp.einsum("rkgd,skd->rkgs", query_block, key_half, preferred_element_type=jnp.float32)
            * score_scale
        )
        return jnp.where(visible[:, None, None, :], raw_score, masked_score)

    def weights_from(scores, visible, offset):
        return jnp.where(visible[:, None, None, :], jnp.exp(scores - offset[..., None]), 0.0)

    def gradient_products(grad_block):
        return jnp.einsum(
            "rkgd,skd->rkgs", grad_block, value_half, preferred_element_type=jnp.float32
        )

    def max_pass(inputs):
        query_block, visible = inputs
        scores = masked_scores(query_block, visible)
        largest = jnp.max(scores, axis=-1)
        return (largest, jnp.sum(weights_from(scores, visible, largest), axis=-1))

    largest, denominator = lax.map(max_pass, (query_blocks, visible_all))
    largest, denominator = merged((largest, denominator), "slot", merge_pairs)
    log_total = largest + jnp.log(denominator)

    def product_pass(inputs):
        query_block, grad_block, visible, block_total = inputs
        probability = weights_from(masked_scores(query_block, visible), visible, block_total)
        return jnp.sum(probability * gradient_products(grad_block), axis=-1)

    partial_sum = lax.map(product_pass, (query_blocks, grad_blocks, visible_all, log_total))
    row_sum = lax.psum(partial_sum, "slot")

    def last_pass(running, inputs):
        key_grad, value_grad = running
        query_block, grad_block, visible, block_total, block_sum = inputs
        probability = weights_from(masked_scores(query_block, visible), visible, block_total)
        prob_grad = gradient_products(grad_block)
        score_grad = (probability * (prob_grad - block_sum[..., None])).astype(jnp.bfloat16)
        prob_half = probability.astype(jnp.bfloat16)
        value_grad = value_grad + jnp.einsum(
            "rkgs,rkgd->skd", prob_half, grad_block, preferred_element_type=jnp.float32
        )
        key_grad = (
            key_grad
            + jnp.einsum(
                "rkgs,rkgd->skd", score_grad, query_block, preferred_element_type=jnp.float32
            )
            * score_scale
        )
        query_part = (
            jnp.einsum("rkgs,skd->rkgd", score_grad, key_half, preferred_element_type=jnp.float32)
            * score_scale
        )
        return ((key_grad, value_grad), query_part)

    empty_grad = jnp.zeros(key_half.shape, jnp.float32)
    (key_grad, value_grad), query_parts = lax.scan(
        last_pass,
        (empty_grad, empty_grad),
        (query_blocks, grad_blocks, visible_all, log_total, row_sum),
    )
    query_terms = query_parts.reshape(total_rows, head_count, head_width)
    summed = lax.psum(query_terms, "slot")
    own_rows = queries.shape[0]
    query_grad = lax.dynamic_slice_in_dim(summed, lax.axis_index("slot") * own_rows, own_rows, 0)
    key_total, value_total = lax.psum((key_grad, value_grad), "conv")
    slot_grad = jnp.stack([key_total, value_total])
    new_first = beta_one * first_moment + (1.0 - beta_one) * slot_grad
    new_second = beta_two * second_moment + (1.0 - beta_two) * slot_grad * slot_grad
    first_fix = 1.0 - beta_one**STEP
    second_fix = 1.0 - beta_two**STEP
    new_cache = cache - learn_rate * (new_first / first_fix) / (
        jnp.sqrt(new_second / second_fix) + adam_eps
    )
    return (new_cache, new_first, new_second, query_grad)


def solution(mesh):
    in_specs = (
        P(("conv", "slot"), "head", None),
        P(("conv", "slot"), "head", None),
        P("conv"),
        P("slot"),
        P(None, "slot", "head", None),
        P(None, "slot", "head", None),
        P(None, "slot", "head", None),
    )
    out_specs = (
        P(None, "slot", "head", None),
        P(None, "slot", "head", None),
        P(None, "slot", "head", None),
        P(("conv", "slot"), "head", None),
    )
    return jax.shard_map(local, mesh=mesh, in_specs=in_specs, out_specs=out_specs, check_vma=False)
```

profile of v0, /device:TPU:1, one launch (start us, length us, event | category | flops | bytes accessed | tf_op | source)
XLA Modules:
  0.0 525.3 jit_solution(10511550598650439508)
XLA Ops:
  13.1 43.8 %all-gather.5.cloned.1.call-done = bf16[256,32,128]{2,1,0:T(8,128)(2,1)} async-done(((bf16[16,32,128]{2,1,0:T(8,128)(2,1)}), bf16[256,32,128]{2,1,0:T(8,128)(2,1)}) %all-gather.5.cloned.1.call-update) | async-done | bytes 2097168 | tf_op jit(solution)/shard_map/all_gather | solution.py:35
  56.9 3.3 copy.50
  60.1 43.2 %all-gather.7.cloned.1.call-done = bf16[256,32,128]{2,1,0:T(8,128)(2,1)} async-done(((bf16[16,32,128]{2,1,0:T(8,128)(2,1)}), bf16[256,32,128]{2,1,0:T(8,128)(2,1)}) %all-gather.7.cloned.1.call-update) | async-done | bytes 2097168 | tf_op jit(solution)/shard_map/all_gather | solution.py:36
  103.3 3.3 copy.51
  106.6 23.2 %while.54 = (s32[]{:T(128)}, f32[4,64,2,16]{1,3,2,0:T(8,128)S(1)}, f32[4,64,2,16]{1,3,2,0:T(8,128)S(1)}, pred[4,64,1024]{2,1,0:T(8,128)(4,1)S(1)}, bf16[4,64,2,1...) while((s32[]{:T(128)}, f32[4,64,2,16]{1,3,2,0:T(8,128)S(1)}, ...), condition=%wide.region_3.4_spmd, body=%wide.region_0.3_spmd.sunk | while | flops 553644032 | bytes 18210912 | solution.py:73
  106.6 2.8 bitcast_reduce_fusion.2
  109.4 2.8 fusion.87
  112.4 2.8 bitcast_reduce_fusion.2
  115.2 2.8 fusion.87
  118.2 2.8 bitcast_reduce_fusion.2
  121.0 2.8 fusion.87
  124.0 2.8 bitcast_reduce_fusion.2
  126.8 2.8 fusion.87
  129.8 19.1 %all-gather.1 = f32[64,64,2,16]{1,3,2,0:T(8,128)S(1)} all-gather(f32[4,64,2,16]{1,3,2,0:T(8,128)S(1)} %get-tuple-element.272), channel_id=3, replica_groups=mesh['slot'=16,'head'=2,'conv'=4] {'slot'}, dimensions={0}, use_global_device_ids=true | all-gather | bytes 557056 | tf_op jit(solution)/shard_map/all_gather | solution.py:16
  148.9 17.4 %all-gather = f32[64,64,2,16]{1,3,2,0:T(8,128)S(1)} all-gather(f32[4,64,2,16]{1,3,2,0:T(8,128)S(1)} %get-tuple-element.271), channel_id=2, replica_groups=mesh['slot'=16,'head'=2,'conv'=4] {'slot'}, dimensions={0}, use_global_device_ids=true | all-gather | bytes 557056 | tf_op jit(solution)/shard_map/all_gather | solution.py:16
  167.2 13.9 %while.55 = (s32[]{:T(128)}, f32[4,64,2,16]{1,3,2,0:T(8,128)S(1)}, f32[4,64,2,16]{1,3,2,0:T(8,128)S(1)}, f32[16,4,64,2,16]{2,4,3,1,0:T(8,128)}, f32[16,4,64,2,16...) while((s32[]{:T(128)}, f32[4,64,2,16]{1,3,2,0:T(8,128)S(1)}, f32[4,64,2,16]{1,3,2,0:T(8,128)S(1)}, ...), condition=%wide.region_5.6_spmd, body=%wide.region_4.5_spmd.sunk | while | flops 49157 | bytes 196731 | solution.py:22
  181.5 31.2 %while.56 = (s32[]{:T(128)}, f32[4,64,2,16]{3,1,2,0:T(8,128)}, pred[4,64,1024]{2,1,0:T(8,128)(4,1)S(1)}, bf16[4,64,2,16,128]{4,3,1,2,0:T(8,128)(2,1)}, bf16[1024...) while((s32[]{:T(128)}, f32[4,64,2,16]{3,1,2,0:T(8,128)}, ...), condition=%wide.region_8.9_spmd, body=%wide.region_6.8_spmd.sunk | while | flops 1086322688 | bytes 21397652 | solution.py:82
  183.9 4.7 fusion.94
  191.7 4.7 fusion.94
  199.5 4.7 fusion.94
  207.3 4.7 fusion.94
  212.7 61.1 %psum.28 = f32[4,64,2,16]{3,1,2,0:T(8,128)S(1)} all-reduce(f32[4,64,2,16]{3,1,2,0:T(8,128)} %get-tuple-element.275), channel_id=1, replica_groups=mesh['slot'=16,'head'=2,'conv'=4] {'slot'}, use_global_device_ids=true, to_apply=%region_9.10 | all-reduce | flops 8192 | bytes 65536 | tf_op jit(solution)/shard_map/psum | solution.py:83
  273.8 52.7 %while.57 = (s32[]{:T(128)}, f32[1024,2,128]{0,2,1:T(8,128)S(1)}, f32[1024,2,128]{0,2,1:T(8,128)S(1)}, f32[4,64,2,16,128]{4,3,2,1,0:T(8,128)}, bf16[4,64,2,16,12...) while((s32[]{:T(128)}, f32[1024,2,128]{0,2,1:T(8,128)S(1)}, ...), condition=%wide.region_11.12_spmd.clone, body=%wide.region_10.11_spmd.clone.sunk | while | flops 2711093248 | bytes 59867360 | solution.py:109
  276.4 2.7 fusion.108
  279.1 3.5 fusion.106
  292.2 3.5 fusion.106
  302.7 2.7 fusion.108
  305.4 3.5 fusion.106
  318.6 3.5 fusion.106
  329.7 81.8 %all-reduce.6.cloned.1.call-done = (f32[1,1024,2,128]{3,2,1,0:T(2,128)}, f32[1,1024,2,128]{3,2,1,0:T(2,128)}) async-done(((f32[1,1024,2,128]{3,2,1,0:T(2,128)}, f32[1,1024,2,128]{3,2,1,0:T(2,128)}), (f32[1,1024,2,128]{3,2,1,0:T(2,128)}, f32[1,1024,2,128]{3,2,1,0:T(2,128)})) %all-reduce.6.cloned.1.call-update) | async-done | bytes 2097168 | tf_op jit(solution)/shard_map/psum | solution.py:118
  414.5 8.0 %divide_subtract_fusion = (f32[2,1024,2,128]{3,2,1,0:T(2,128)}, f32[2,1024,2,128]{3,2,1,0:T(2,128)}, f32[2,1024,2,128]{3,2,1,0:T(2,128)}) fusion(f32[2,1024,2,128]{3,2,1,0:T(2,128)S(1)} %copy-done, f32[2,1024,2,128]{3,2,1,0:T(2,128)S(1)} %constant_dynamic-update-slice_fusion.2, f32[2,1024,2,128]{3,2,1,0:T(2,128)S(1)} %copy-done.1, ...), kind=kLoop, calls=%fused_computation.80 | loop fusion | flops 6291456 | bytes 14680064 | tf_op jit(solution)/shard_map/sub | solution.py:124
  422.5 94.6 %all-reduce.4.cloned.1.call-done = f32[256,32,128]{2,1,0:T(8,128)} async-done(((f32[256,32,128]{2,1,0:T(8,128)}), f32[256,32,128]{2,1,0:T(8,128)}) %all-reduce.4.cloned.1.call-update) | async-done | bytes 4194320 | tf_op jit(solution)/shard_map/psum | solution.py:115
  (135 shorter events, 74.4 us)
Async XLA Ops:
  7.2 49.7 %all-gather.5.cloned.1.call-start = ((), (), s32[]{:S(2)}) async-start(), calls=%async_computation | async-start | bytes 2228224 | tf_op jit(solution)/shard_map/all_gather | solution.py:35
  7.9 95.4 %all-gather.7.cloned.1.call-start = ((), (), s32[]{:S(2)}) async-start(), calls=%async_computation.1 | async-start | bytes 2228224 | tf_op jit(solution)/shard_map/all_gather | solution.py:36
  8.6 402.9 %all-reduce.6.cloned.1.call-start = ((), (), s32[]{:S(2)}) async-start(), calls=%async_computation.3 | async-start | bytes 4194304 | tf_op jit(solution)/shard_map/psum | solution.py:118
  166.2 1.0 copy-start.4
  181.4 92.4 %copy-start.5 = (f32[1024,2,128]{0,2,1:T(8,128)S(1)}, f32[1024,2,128]{0,2,1:T(8,128)}, u32[]{:S(2)}) copy-start(f32[1024,2,128]{0,2,1:T(8,128)} %custom-call.1) | copy-start | bytes 3145732
  181.5 2.4 copy-start.6
  189.3 2.4 copy-start.6
  197.1 2.4 copy-start.6
  204.9 2.4 copy-start.6
  273.9 2.5 copy-start.3
  276.4 2.7 copy-start.7
  287.1 2.5 copy-start.3
  289.5 2.7 copy-start.7
  300.3 2.5 copy-start.3
  302.7 2.7 copy-start.7
  313.4 2.5 copy-start.3
  315.9 2.7 copy-start.7
  329.2 187.9 %all-reduce.4.cloned.1.call-start = ((), (), s32[]{:S(2)}) async-start(), calls=%async_computation.2 | async-start | bytes 8388608 | tf_op jit(solution)/shard_map/psum | solution.py:115
  329.2 85.2 %copy-start = (f32[2,1024,2,128]{3,2,1,0:T(2,128)S(1)}, f32[2,1024,2,128]{3,2,1,0:T(2,128)}, u32[]{:S(2)}) copy-start(f32[2,1024,2,128]{3,2,1,0:T(2,128)} %param.19) | copy-start | bytes 6291460
  411.5 3.0 copy-start.1
  411.5 3.0 copy-start.2
Sparse Core Ops, SparseCore 0:
  10.1 46.6 all-gather.4
  59.0 44.2 all-gather.6
  329.3 82.1 all-reduce.5
  414.7 102.2 all-reduce.3
where the time goes:
time: 527 us; the launch traced here: 525 us
  waiting for transfers between devices  265 us (50%)
  blocking collectives  97.6 us (19%)
  matrix products  87.3 us (17%)
  other arithmetic  33.9 us (6%)
  local copies, waits for them, and re-layouts  26.4 us (5%)
  between operations  13.9 us (3%)
    psum x1, waiting for transfers between devices, local(): summed = lax.psum(query_terms, 'slot')  94.6 us
    psum x1, waiting for transfers between devices, local(): key_total, value_total = lax.psum((key_grad, value_grad), 'conv')  81.8 us
    psum x1, blocking collectives, local(): row_sum = lax.psum(partial_sum, 'slot')  61.1 us
    all_gather x1, waiting for transfers between devices, local(): lax.all_gather(queries, 'slot', axis=0, tiled=True)  43.8 us
    all_gather x1, waiting for transfers between devices, local(): lax.all_gather(out_grad, 'slot', axis=0, tiled=True)  43.2 us
    all_gather x2, blocking collectives, merged(): everything = jax.tree.map(lambda part: lax.all_gather(part, axis), x)  36.5 us
    dot_general x8, matrix products, gradient_products(): jnp.einsum('rkgd,skd->rkgs', grad_block, value_half, preferred_element_ty...  32.8 us
    dot_general x12, matrix products, masked_scores(): jnp.einsum('rkgd,skd->rkgs', query_block, key_half, preferred_element_typ...  30.3 us
  transfers between devices with their start and end apart: 4, of which 4 were waited for; matrix products, arithmetic and copies ran while one was open for 4% of the time, Pallas kernels for 0%

commit v1 on v0

--- a/solution.py
+++ b/solution.py
@@ -80,7 +80,7 @@
         return jnp.sum(probability * gradient_products(grad_block), axis=-1)
 
     partial_sum = lax.map(product_pass, (query_blocks, grad_blocks, visible_all, log_total))
-    row_sum = lax.psum(partial_sum, "slot")
+    row_sum = jnp.sum(lax.all_gather(partial_sum, "slot"), axis=0)
 
     def last_pass(running, inputs):
         key_grad, value_grad = running

time: 527 us -> 479 us (0.909)
  blocking collectives: 97.6 us -> 55.6 us
  waiting for transfers between devices: 265 us -> 257 us
    psum x1 -> x0, blocking collectives: 61.1 us -> none  [local(): row_sum = lax.psum(partial_sum, 'slot')]
    all_gather x0 -> x1, blocking collectives: none -> 19 us  [local(): row_sum = jnp.sum(lax.all_gather(partial_sum, 'slot'), axis=0)]
    psum x1, waiting for transfers between devices: 81.8 us -> 73.8 us  [local(): key_total, value_total = lax.psum((key_grad, value_grad), 'conv')]
where the time goes in v1:
time: 479 us; the launch traced here: 477 us
  waiting for transfers between devices  257 us (54%)
  matrix products  86.9 us (18%)
  blocking collectives  55.6 us (12%)
  other arithmetic  35.8 us (7%)
  local copies, waits for them, and re-layouts  27.1 us (6%)
  between operations  13.9 us (3%)
    psum x1, waiting for transfers between devices, local(): summed = lax.psum(query_terms, 'slot')  93.1 us
    psum x1, waiting for transfers between devices, local(): key_total, value_total = lax.psum((key_grad, value_grad), 'conv')  73.8 us
    all_gather x1, waiting for transfers between devices, local(): lax.all_gather(queries, 'slot', axis=0, tiled=True)  44.6 us
    all_gather x1, waiting for transfers between devices, local(): lax.all_gather(out_grad, 'slot', axis=0, tiled=True)  43.2 us
    all_gather x2, blocking collectives, merged(): everything = jax.tree.map(lambda part: lax.all_gather(part, axis), x)  36.6 us
    dot_general x8, matrix products, gradient_products(): jnp.einsum('rkgd,skd->rkgs', grad_block, value_half, preferred_element_ty...  32.7 us
    dot_general x12, matrix products, masked_scores(): jnp.einsum('rkgd,skd->rkgs', query_block, key_half, preferred_element_typ...  30.1 us
    all_gather x1, blocking collectives, local(): row_sum = jnp.sum(lax.all_gather(partial_sum, 'slot'), axis=0)  19 us
  transfers between devices with their start and end apart: 4, of which 4 were waited for; matrix products, arithmetic and copies ran while one was open for 4% of the time, Pallas kernels for 0%

profile of v1, /device:TPU:1, one launch (start us, length us, event | category | flops | bytes accessed | tf_op | source)
XLA Modules:
  0.0 477.0 jit_solution(2266693866155780145)
XLA Ops:
  12.2 44.6 %all-gather.6.cloned.1.call-done = bf16[256,32,128]{2,1,0:T(8,128)(2,1)} async-done(((bf16[16,32,128]{2,1,0:T(8,128)(2,1)}), bf16[256,32,128]{2,1,0:T(8,128)(2,1)}) %all-gather.6.cloned.1.call-update) | async-done | bytes 2097168 | tf_op jit(solution)/shard_map/all_gather | solution.py:35
  56.9 3.3 copy.49
  60.1 43.2 %all-gather.8.cloned.1.call-done = bf16[256,32,128]{2,1,0:T(8,128)(2,1)} async-done(((bf16[16,32,128]{2,1,0:T(8,128)(2,1)}), bf16[256,32,128]{2,1,0:T(8,128)(2,1)}) %all-gather.8.cloned.1.call-update) | async-done | bytes 2097168 | tf_op jit(solution)/shard_map/all_gather | solution.py:36
  103.3 3.3 copy.50
  106.6 23.2 %while.54 = (s32[]{:T(128)}, f32[4,64,2,16]{1,3,2,0:T(8,128)S(1)}, f32[4,64,2,16]{1,3,2,0:T(8,128)S(1)}, pred[4,64,1024]{2,1,0:T(8,128)(4,1)S(1)}, bf16[4,64,2,1...) while((s32[]{:T(128)}, f32[4,64,2,16]{1,3,2,0:T(8,128)S(1)}, ...), condition=%wide.region_3.4_spmd, body=%wide.region_0.3_spmd.sunk | while | flops 553644032 | bytes 18210912 | solution.py:73
  106.6 2.8 bitcast_reduce_fusion.2
  109.4 2.8 fusion.87
  112.4 2.8 bitcast_reduce_fusion.2
  115.2 2.8 fusion.87
  118.2 2.8 bitcast_reduce_fusion.2
  121.0 2.8 fusion.87
  124.0 2.8 bitcast_reduce_fusion.2
  126.8 2.8 fusion.87
  131.1 19.1 %all-gather.1 = f32[64,64,2,16]{1,3,2,0:T(8,128)S(1)} all-gather(f32[4,64,2,16]{1,3,2,0:T(8,128)} %copy-done.6), channel_id=3, replica_groups=mesh['slot'=16,'head'=2,'conv'=4] {'slot'}, dimensions={0}, use_global_device_ids=true | all-gather | bytes 557056 | tf_op jit(solution)/shard_map/all_gather | solution.py:16
  150.2 17.5 %all-gather = f32[64,64,2,16]{1,3,2,0:T(8,128)S(1)} all-gather(f32[4,64,2,16]{1,3,2,0:T(8,128)} %copy-done.7), channel_id=2, replica_groups=mesh['slot'=16,'head'=2,'conv'=4] {'slot'}, dimensions={0}, use_global_device_ids=true | all-gather | bytes 557056 | tf_op jit(solution)/shard_map/all_gather | solution.py:16
  168.6 13.9 %while.55 = (s32[]{:T(128)}, f32[4,64,2,16]{1,3,2,0:T(8,128)S(1)}, f32[4,64,2,16]{1,3,2,0:T(8,128)S(1)}, f32[16,4,64,2,16]{2,4,3,1,0:T(8,128)}, f32[16,4,64,2,16...) while((s32[]{:T(128)}, f32[4,64,2,16]{1,3,2,0:T(8,128)S(1)}, f32[4,64,2,16]{1,3,2,0:T(8,128)S(1)}, ...), condition=%wide.region_5.6_spmd, body=%wide.region_4.5_spmd.sunk | while | flops 49157 | bytes 196731 | solution.py:22
  182.9 28.5 %while.56 = (s32[]{:T(128)}, f32[4,64,2,16]{1,3,2,0:T(8,128)S(1)}, pred[4,64,1024]{2,1,0:T(8,128)(4,1)S(1)}, bf16[4,64,2,16,128]{4,3,1,2,0:T(8,128)(2,1)}, bf16[...) while((s32[]{:T(128)}, f32[4,64,2,16]{1,3,2,0:T(8,128)S(1)}, ...), condition=%wide.region_8.9_spmd, body=%wide.region_6.8_spmd.sunk | while | flops 1086322688 | bytes 19275896 | solution.py:82
  185.2 4.7 fusion.94
  192.4 4.7 fusion.94
  199.5 4.7 fusion.94
  206.6 4.7 fusion.94
  212.8 19.0 %all-gather.2 = f32[64,64,2,16]{1,3,2,0:T(8,128)S(1)} all-gather(f32[4,64,2,16]{1,3,2,0:T(8,128)} %copy-done.8), channel_id=4, replica_groups=mesh['slot'=16,'head'=2,'conv'=4] {'slot'}, dimensions={0}, use_global_device_ids=true | all-gather | bytes 557056 | tf_op jit(solution)/shard_map/all_gather | solution.py:83
  232.0 53.3 %while.57 = (s32[]{:T(128)}, f32[1024,2,128]{0,2,1:T(8,128)S(1)}, f32[1024,2,128]{0,2,1:T(8,128)}, f32[4,64,2,16,128]{4,3,2,1,0:T(8,128)}, bf16[4,64,2,16,128]{4...) while((s32[]{:T(128)}, f32[1024,2,128]{0,2,1:T(8,128)S(1)}, ...), condition=%wide.region_11.12_spmd.clone, body=%wide.region_10.11_spmd.clone.sunk | while | flops 2711093248 | bytes 68272416 | solution.py:109
  234.6 2.7 fusion.108
  237.3 3.5 fusion.106
  250.6 3.5 fusion.106
  261.3 2.7 fusion.108
  264.0 3.5 fusion.106
  277.3 3.5 fusion.106
  289.4 73.8 %all-reduce.6.cloned.1.call-done = (f32[1,1024,2,128]{3,2,1,0:T(2,128)}, f32[1,1024,2,128]{3,2,1,0:T(2,128)}) async-done(((f32[1,1024,2,128]{3,2,1,0:T(2,128)}, f32[1,1024,2,128]{3,2,1,0:T(2,128)}), (f32[1,1024,2,128]{3,2,1,0:T(2,128)}, f32[1,1024,2,128]{3,2,1,0:T(2,128)})) %all-reduce.6.cloned.1.call-update) | async-done | bytes 2097168 | tf_op jit(solution)/shard_map/psum | solution.py:118
  365.9 9.8 %divide_subtract_fusion = (f32[2,1024,2,128]{3,2,1,0:T(2,128)}, f32[2,1024,2,128]{3,2,1,0:T(2,128)}, f32[2,1024,2,128]{3,2,1,0:T(2,128)}) fusion(f32[2,1024,2,128]{3,2,1,0:T(2,128)} %param.19, f32[2,1024,2,128]{3,2,1,0:T(2,128)S(1)} %constant_dynamic-update-slice_fusion.3, f32[2,1024,2,128]{3,2,1,0:T(2,128)} %param.20, f32[2,1024,2,128]{3,2,1,0:T(2,128)} %param.21), kind=kLoop, calls=%fused_computation.80 | loop fusion | flops 6291456 | bytes 14680064 | tf_op jit(solution)/shard_map/sub | solution.py:124
  375.7 93.1 %all-reduce.4.cloned.1.call-done = f32[256,32,128]{2,1,0:T(8,128)} async-done(((f32[256,32,128]{2,1,0:T(8,128)}), f32[256,32,128]{2,1,0:T(8,128)}) %all-reduce.4.cloned.1.call-update) | async-done | bytes 4194320 | tf_op jit(solution)/shard_map/psum | solution.py:115
  (156 shorter events, 75.0 us)
Async XLA Ops:
  7.2 49.7 %all-gather.6.cloned.1.call-start = ((), (), s32[]{:S(2)}) async-start(), calls=%async_computation | async-start | bytes 2228224 | tf_op jit(solution)/shard_map/all_gather | solution.py:35
  7.9 95.4 %all-gather.8.cloned.1.call-start = ((), (), s32[]{:S(2)}) async-start(), calls=%async_computation.1 | async-start | bytes 2228224 | tf_op jit(solution)/shard_map/all_gather | solution.py:36
  8.6 354.6 %all-reduce.6.cloned.1.call-start = ((), (), s32[]{:S(2)}) async-start(), calls=%async_computation.3 | async-start | bytes 4194304 | tf_op jit(solution)/shard_map/psum | solution.py:118
  129.8 0.6 copy-start.6
  130.4 0.6 copy-start.7
  167.6 1.0 copy-start.1
  211.4 0.8 copy-start.4
  212.2 0.6 copy-start.8
  232.1 2.5 copy-start
  232.1 2.5 copy-start.2
  234.6 2.7 copy-start.5
  237.3 3.5 copy-start.3
  245.4 2.5 copy-start
  245.4 2.5 copy-start.2
  247.9 2.7 copy-start.5
  250.6 3.5 copy-start.3
  258.8 2.5 copy-start
  258.8 2.5 copy-start.2
  261.3 2.7 copy-start.5
  264.0 3.5 copy-start.3
  272.1 2.5 copy-start
  272.1 2.5 copy-start.2
  274.6 2.7 copy-start.5
  277.3 3.5 copy-start.3
  288.9 180.0 %all-reduce.4.cloned.1.call-start = ((), (), s32[]{:S(2)}) async-start(), calls=%async_computation.2 | async-start | bytes 8388608 | tf_op jit(solution)/shard_map/psum | solution.py:115
Sparse Core Ops, SparseCore 0:
  10.1 46.6 all-gather.5
  59.0 44.2 all-gather.7
  289.0 74.2 all-reduce.5
  366.5 102.2 all-reduce.3
